TPU v7x, 256 devices: a whole 4x4x8 slice. The times are simulated.
256 devices in a mesh: dp: 64 (over z, x, core), head: 4 (over y).
Axes of the slice: x: 4, y: 4, z: 8, core: 2. Of those that a mesh axis runs over, the one named last changes fastest.
Arguments:
- queries: bfloat16 [32768, 2048], P('dp', 'head'), may hold values from -48 to 48
- encodings: bfloat16 [1024, 128, 896], P('dp', None, 'head'), may hold values from -12 to 12
- neighbour_ids: int32 [512, 2], P('dp'), may hold values from 0 to 1023, as said below
- block_place: int32 [1024], replicated, may hold values from 0 to 1023, as said below
- query_weight: bfloat16 [4096, 2048], P(None, 'head'), may hold values from -1 to 1
- key_weight: bfloat16 [896, 2048], P(None, 'head'), may hold values from -1 to 1
- value_weight: bfloat16 [896, 2048], P(None, 'head'), may hold values from -0.1875 to 0.1875
- attn_grad: bfloat16 [32768, 2048], P('dp', 'head'), may hold values from -24 to 24
Outputs:
- query_input_grad: bfloat16 [32768, 4096], P('dp', 'head')
- encodings_grad: bfloat16 [1024, 128, 896], P('dp', None, 'head')
- key_weight_grad: float32 [896, 2048], P('dp', 'head')
- value_weight_grad: float32 [896, 2048], P('dp', 'head')
Inputs may be any that keep to these rules, and one draw needn't show every extreme that they name: `neighbour_ids`: block b is stored at position block_place[b] of encodings, on the index block_place[b] // 16 of dp. Of the 16 slots of the spans of one index of dp, each index of dp stores the blocks of 1 or 0, and some index stores those of exactly 1. `block_place`: A permutation: every position once.
All inputs are finite; a program needn't handle non-finite values.
Results may differ from a plain program's by a relative error of at most 0.012.
The roundings to bfloat16 on the way count: a program that leaves them out, or rounds other values in their place, can miss the bound.
Values may be sent and summed in bfloat16 or wider, within the bound.
No kernel may reach another device: no remote copies, remote signals or barrier semaphores. Data moves between devices by JAX's collectives and lax.ppermute only.
A program may use at most 128 MiB of HBM per device.

v0:
```python
import math
import jax
import jax.numpy as jnp
from jax import lax
from jax.sharding import PartitionSpec as P

DH = 128
E = 896
CH = 64
NTOK = 128
NEIGH = 2


def shards(
    queries,
    encodings,
    neighbour_ids,
    block_place,
    query_weight,
    key_weight,
    value_weight,
    attn_grad,
):
    dp_count = lax.axis_size("dp")
    own_blocks = encodings.shape[0]
    span_count = neighbour_ids.shape[0]
    block_names = neighbour_ids.reshape(-1)
    slot_count = block_names.shape[0]
    capacity = -(-slot_count // dp_count)
    position = block_place[block_names]
    owner_dev = position // own_blocks
    local_slot = position % own_blocks
    slot_order = jnp.arange(slot_count, dtype=jnp.int32)
    same_owner = (owner_dev[:, None] == owner_dev[None, :]) & (
        slot_order[None, :] < slot_order[:, None]
    )
    slot_rank = jnp.sum(same_owner.astype(jnp.int32), axis=1)
    device_match = owner_dev[:, None, None] == jnp.arange(dp_count, dtype=jnp.int32)[None, :, None]
    rank_match = slot_rank[:, None, None] == jnp.arange(capacity, dtype=jnp.int32)[None, None, :]
    requests = (
        jnp.sum(jnp.where(device_match & rank_match, local_slot[:, None, None] + 1, 0), axis=0) - 1
    )
    asked_rows = lax.all_to_all(requests, "dp", split_axis=0, concat_axis=0, tiled=True)
    valid_mask = asked_rows >= 0
    local_index = jnp.maximum(asked_rows, 0)
    blank = jnp.zeros((), jnp.bfloat16)
    whole_own = lax.all_gather(encodings, "head", axis=2, tiled=True)
    packed = jnp.where(valid_mask[:, :, None, None], whole_own[local_index], blank)
    received = lax.all_to_all(packed, "dp", split_axis=0, concat_axis=0, tiled=True)
    slot_blocks = received[owner_dev, slot_rank]
    flat_rows = slot_blocks.reshape(-1, E)
    both_weights = jnp.concatenate([key_weight, value_weight], axis=1)
    head_cols = key_weight.shape[1]
    local_heads = head_cols // DH
    projected = jnp.dot(flat_rows, both_weights, preferred_element_type=jnp.float32).astype(
        jnp.bfloat16
    )
    key_rows = projected[:, :head_cols].reshape(span_count, NEIGH * NTOK, local_heads, DH)
    value_rows = projected[:, head_cols:].reshape(span_count, NEIGH * NTOK, local_heads, DH)
    query_heads = queries.reshape(span_count, CH, local_heads, DH)
    grad_heads = attn_grad.reshape(span_count, CH, local_heads, DH)
    score_scale = 1.0 / math.sqrt(DH)
    scores = (
        jnp.einsum("cqhd,ckhd->chqk", query_heads, key_rows, preferred_element_type=jnp.float32)
        * score_scale
    )
    shifted = jnp.exp(scores - jnp.max(scores, axis=-1, keepdims=True))
    prob_rows = shifted / jnp.sum(shifted, axis=-1, keepdims=True)
    prob_half = prob_rows.astype(jnp.bfloat16)
    grad_probs = jnp.einsum(
        "cqhd,ckhd->chqk", grad_heads, value_rows, preferred_element_type=jnp.float32
    )
    row_delta = jnp.sum(prob_rows * grad_probs, axis=-1, keepdims=True)
    grad_scores = (prob_rows * (grad_probs - row_delta) * score_scale).astype(jnp.bfloat16)
    value_grad = jnp.einsum(
        "chqk,cqhd->ckhd", prob_half, grad_heads, preferred_element_type=jnp.float32
    ).astype(jnp.bfloat16)
    key_grad = jnp.einsum(
        "chqk,cqhd->ckhd", grad_scores, query_heads, preferred_element_type=jnp.float32
    ).astype(jnp.bfloat16)
    query_grad = jnp.einsum(
        "chqk,ckhd->cqhd", grad_scores, key_rows, preferred_element_type=jnp.float32
    ).astype(jnp.bfloat16)
    partial_input = jnp.dot(
        query_grad.reshape(-1, head_cols), query_weight.T, preferred_element_type=jnp.float32
    )
    query_input_grad = lax.psum_scatter(
        partial_input.astype(jnp.bfloat16), "head", scatter_dimension=1, tiled=True
    )
    both_grads = jnp.concatenate(
        [key_grad.reshape(-1, head_cols), value_grad.reshape(-1, head_cols)], axis=1
    )
    weight_grads = lax.psum_scatter(
        lax.dot_general(
            flat_rows, both_grads, (((0,), (0,)), ((), ())), preferred_element_type=jnp.float32
        ),
        "dp",
        scatter_dimension=0,
        tiled=True,
    )
    slot_partial = jnp.dot(both_grads, both_weights.T, preferred_element_type=jnp.float32).reshape(
        slot_count, NTOK, E
    )
    slot_grad = lax.psum_scatter(
        slot_partial.astype(jnp.bfloat16), "head", scatter_dimension=2, tiled=True
    )
    quarter = slot_grad.shape[2]
    outgoing = (
        jnp.zeros((dp_count, capacity, NTOK, quarter), jnp.bfloat16)
        .at[owner_dev, slot_rank]
        .set(slot_grad)
    )
    returned = lax.all_to_all(outgoing, "dp", split_axis=0, concat_axis=0, tiled=True)
    block_match = (
        local_index.reshape(-1)[None, :] == jnp.arange(own_blocks, dtype=jnp.int32)[:, None]
    )
    target = (block_match & valid_mask.reshape(-1)[None, :]).astype(jnp.bfloat16)
    encodings_grad = jnp.dot(
        target, returned.reshape(dp_count * capacity, -1), preferred_element_type=jnp.float32
    )
    encodings_grad = encodings_grad.reshape(own_blocks, NTOK, quarter).astype(jnp.bfloat16)
    return (
        query_input_grad,
        encodings_grad,
        weight_grads[:, :head_cols],
        weight_grads[:, head_cols:],
    )


def solution(mesh):
    in_specs = (
        P("dp", "head"),
        P("dp", None, "head"),
        P("dp", None),
        P(),
        P(None, "head"),
        P(None, "head"),
        P(None, "head"),
        P("dp", "head"),
    )
    out_specs = (P("dp", "head"), P("dp", None, "head"), P("dp", "head"), P("dp", "head"))
    return jax.shard_map(shards, mesh=mesh, in_specs=in_specs, out_specs=out_specs, check_vma=False)
```

profile of v0, /device:TPU:1, one launch (start us, length us, event | category | flops | bytes accessed | tf_op | source)
XLA Modules:
  0.0 850.1 jit_solution(8906431637875091830)
XLA Ops:
  7.2 0.0 all-gather.2.cloned.1.call-start
  7.2 2.5 copy.111
  9.7 0.0 all-gather.2.cloned.1.call-update
  9.7 0.1 copy.109
  9.8 0.1 reshape.337
  9.9 0.6 gather_fusion
  10.6 0.2 convert_reduce_fusion
  10.8 0.1 select_reduce_fusion
  10.9 0.1 copy.110
  11.0 22.2 %all_to_all.16 = s32[64,1,1]{2,1,0:T(1,128)S(1)} all-to-all(s32[64,1,1]{2,1,0:T(1,128)S(1)} %copy.110), channel_id=1, replica_groups=mesh['dp'=64,'head'=4] {'dp'}, dimensions={0} | all-to-all | bytes 512 | tf_op jit(solution)/shard_map/all_to_all | solution.py:43
  33.1 1.2 maximum_reduce_fusion
  34.4 1.2 compare_reduce_fusion
  35.6 24.8 %all-gather.2.cloned.1.call-done = bf16[16,128,896]{1,0,2:T(8,128)(2,1)} async-done(((bf16[16,128,224]{1,0,2:T(8,128)(2,1)}), bf16[16,128,896]{1,0,2:T(8,128)(2,1)}) %all-gather.2.cloned.1.call-update) | async-done | bytes 3670032 | tf_op jit(solution)/shard_map/all_gather | solution.py:47
  60.5 6.5 copy.112
  66.9 10.0 %gather_fusion.1 = bf16[64,128,896]{2,1,0:T(8,128)(2,1)} fusion(bf16[16,128,896]{2,1,0:T(8,128)(2,1)} %copy.112, s32[1024]{0:T(1024)S(1)} %pad_clamp_fusion), kind=kCustom, calls=%fused_computation.1 | custom fusion | bytes 29360384 | tf_op jit(solution)/shard_map/gather | solution.py:48
  76.9 13.5 %fusion.2 = bf16[64,1,128,896]{3,2,1,0:T(8,128)(2,1)} fusion(bf16[64,128,896]{2,1,0:T(8,128)(2,1)} %gather_fusion.1, pred[64]{0:T(512)(128)(4,1)S(1)} %compare_reduce_fusion), kind=kLoop, calls=%fused_computation.7 | loop fusion | flops 7340032 | bytes 29360192 | tf_op jit(solution)/shard_map/jit(_where)/select_n | solution.py:48
  90.4 11.3 %all-to-all-start.1 = ((bf16[64,1,128,896]{3,2,1,0:T(8,128)(2,1)}), bf16[64,1,128,896]{3,2,1,0:T(8,128)(2,1)}, u32[]{:S(2)}, u32[]{:S(2)}) async-start(bf16[64,1,128,896]{3,2,1,0:T(8,128)(2,1)} %fusion.2), calls=%async_computation.1 | async-start | bytes 29360128 | tf_op jit(solution)/shard_map/all_to_all | solution.py:49
  101.8 0.0 reduce-scatter.5.cloned.1.call-start
  101.8 0.1 reshape.340
  102.0 1.3 reshape.342
  103.2 0.1 constant_dynamic-update-slice_fusion.1
  103.4 0.1 constant_dynamic-update-slice_fusion
  103.5 1.3 copy-done.9
  104.8 317.0 %all-to-all-done.1 = bf16[64,1,128,896]{3,2,1,0:T(8,128)(2,1)} async-done(((bf16[64,1,128,896]{3,2,1,0:T(8,128)(2,1)}), bf16[64,1,128,896]{3,2,1,0:T(8,128)(2,1)}, u32[]{:S(2)}, u32[]{:S(2)}) %all-to-all-start.1) | async-done | bytes 14680096 | tf_op jit(solution)/shard_map/all_to_all | solution.py:49
  421.8 8.1 gather_fusion.2
  429.9 6.9 convolution_convert_fusion.1
  436.8 2.2 fusion.51
  439.1 2.5 reshape.339
  441.6 0.8 fusion.13
  442.5 2.2 fusion.53
  444.7 4.0 reshape.341
  448.6 3.8 fusion.8
  452.4 7.9 convert_bitcast_fusion
  460.3 17.2 %convert_bitcast_fusion.1 = bf16[8,256,4,128]{3,1,2,0:T(8,128)(2,1)} fusion(f32[8,4,256,64]{2,3,1,0:T(8,128)} %fusion.8, bf16[8,64,4,128]{3,2,1,0:T(4,128)(2,1)S(1)} %reshape.340, f32[8,4,64,256]{3,2,1,0:T(8,128)} %get-tuple-element.41, f32[8,4,64]{2,1,0:T(4,128)S(1)} %get-tuple-element.40), kind=kOutput, calls=%fused_computation.23 | convolution fusion | flops 138938624 | bytes 6823936 | tf_op jit(solution)/shard_map/chqk,cqhd->ckhd/dot_general | solution.py:78
  477.5 4.5 copy.121
  482.0 2.3 copy.130
  484.3 1.5 constant_dynamic-update-slice_fusion.3
  485.7 4.5 copy.123
  490.3 2.4 copy.131
  492.7 0.4 copy-done.4
  493.1 0.1 constant_dynamic-update-slice_fusion.2
  493.2 1.4 copy-done.11
  494.6 6.2 convolution_convert_fusion.2
  500.8 6.1 copy.124
  506.9 0.0 all-reduce.3.cloned.1.call-start
  506.9 9.1 %fusion.54 = f32[896,1024]{1,0:T(8,128)} fusion(bf16[2048,896]{1,0:T(8,128)(2,1)} %bitcast.125, bf16[2048,1024]{0,1:T(8,128)(2,1)} %copy-done.5), kind=kOutput, calls=%fused_computation.90 | convolution fusion | flops 3758096384 | bytes 11534336 | tf_op jit(solution)/shard_map/dot_general | solution.py:94
  516.1 0.0 reduce-scatter.3.cloned.1.call-start
  516.1 14.8 %fusion.20 = bf16[8,64,4,128]{3,1,2,0:T(8,128)(2,1)S(1)} fusion(bf16[8,256,4,128]{3,2,1,0:T(4,128)(2,1)S(1)} %reshape.339, f32[8,4,256,64]{2,3,1,0:T(8,128)} %fusion.8, f32[8,4,64,256]{3,2,1,0:T(8,128)} %get-tuple-element.41, f32[8,4,64]{2,1,0:T(4,128)S(1)} %get-tuple-element.40), kind=kOutput, calls=%fused_computation.31 | convolution fusion | flops 138152192 | bytes 6823936 | tf_op jit(solution)/shard_map/chqk,ckhd->cqhd/dot_general | solution.py:81
  531.0 0.4 copy.119
  531.4 6.5 convolution_convert_fusion
  537.9 15.2 %reduce-scatter.5.cloned.1.call-done = bf16[16,128,224]{1,2,0:T(8,128)(2,1)} async-done(((bf16[16,128,896]{1,2,0:T(8,128)(2,1)}), bf16[16,128,224]{1,2,0:T(8,128)(2,1)}) %reduce-scatter.5.cloned.1.call-update) | async-done | bytes 917520 | tf_op jit(solution)/shard_map/reduce_scatter | solution.py:104
  553.2 2.3 broadcast.388
  555.4 2.9 scatter_fusion
  558.4 11.0 %all-to-all-start.2 = ((bf16[64,1,128,224]{2,3,1,0:T(8,128)(2,1)}), bf16[64,1,128,224]{2,3,1,0:T(8,128)(2,1)}, u32[]{:S(2)}, u32[]{:S(2)}) async-start(bf16[64,1,128,224]{2,3,1,0:T(8,128)(2,1)} %bitcast.117), calls=%async_computation.4 | async-start | bytes 7340032 | tf_op jit(solution)/shard_map/all_to_all | solution.py:113
  569.4 0.6 dynamic-slice
  570.6 219.8 %all-reduce.3.cloned.1.call-done = f32[896,1024]{1,0:T(8,128)} async-done(((f32[896,1024]{1,0:T(8,128)}), f32[896,1024]{1,0:T(8,128)}) %all-reduce.3.cloned.1.call-update) | async-done | bytes 3670032
  790.4 1.5 fusion.52
  791.9 6.2 copy.126
  798.1 9.7 %reshape.346 = bf16[64,28672]{1,0:T(8,128)(2,1)} reshape(bf16[64,1,128,224]{3,2,0,1:T(8,128)(2,1)} %copy.126) | data formatting | bytes 7340032 | tf_op jit(solution)/shard_map/reshape | solution.py:119
  807.8 8.0 dot_general.46
  815.9 6.6 copy.127
  822.4 2.7 convolution_convert_fusion.3
  825.1 1.2 copy.128
  826.3 16.9 %reduce-scatter.3.cloned.1.call-done = bf16[512,1024]{1,0:T(8,128)(2,1)} async-done(((bf16[512,4096]{1,0:T(8,128)(2,1)}), bf16[512,1024]{1,0:T(8,128)(2,1)}) %reduce-scatter.3.cloned.1.call-update) | async-done | bytes 1048592 | tf_op jit(solution)/shard_map/reduce_scatter | solution.py:87
  (36 shorter events, 0.2 us)
Async XLA Ops:
  7.2 2.7 copy-start
  7.2 2.5 copy-start.12
  7.2 53.3 %all-gather.2.cloned.1.call-start = ((), (), s32[]{:S(2)}) async-start(), calls=%async_computation.5 | async-start | bytes 4587520 | tf_op jit(solution)/shard_map/all_gather | solution.py:47
  90.4 11.4 %copy-start.8 = (bf16[512,512]{1,0:T(8,128)(2,1)S(1)}, bf16[512,512]{1,0:T(8,128)(2,1)}, u32[]{:S(2)}) copy-start(bf16[512,512]{1,0:T(8,128)(2,1)} %param.8) | copy-start | bytes 1572868
  90.4 331.4 %all-to-all-start.1 = ((bf16[64,1,128,896]{3,2,1,0:T(8,128)(2,1)}), bf16[64,1,128,896]{3,2,1,0:T(8,128)(2,1)}, u32[]{:S(2)}, u32[]{:S(2)}) async-start(bf16[64,1,128,896]{3,2,1,0:T(8,128)(2,1)} %fusion.2), calls=%async_computation.1 | async-start | bytes 29360128 | tf_op jit(solution)/shard_map/all_to_all | solution.py:49
  101.7 1.5 copy-start.6
  101.8 1.6 copy-start.7
  101.8 451.4 %reduce-scatter.5.cloned.1.call-start = ((), (), s32[]{:S(2)}) async-start(), calls=%async_computation.7 | async-start | bytes 4587520 | tf_op jit(solution)/shard_map/reduce_scatter | solution.py:104
  103.5 1.3 copy-start.9
  421.8 8.1 copy-start.10
  442.5 2.2 copy-start.2
  490.3 2.8 copy-start.4
  493.1 1.5 copy-start.11
  494.6 6.2 copy-start.5
  506.9 283.5 %all-reduce.3.cloned.1.call-start = ((), (), s32[]{:S(2)}) async-start(), calls=%async_computation.8 | async-start | bytes 7340032
  516.1 327.1 %reduce-scatter.3.cloned.1.call-start = ((), (), s32[]{:S(2)}) async-start(), calls=%async_computation.6 | async-start | bytes 5242880 | tf_op jit(solution)/shard_map/reduce_scatter | solution.py:87
  553.1 2.3 copy-start.3
  558.4 11.0 %copy-start.13 = (u32[256]{0:T(256)S(1)}, u32[256]{0:T(256)}, u32[]{:S(2)}) copy-start(u32[256]{0:T(256)} %constant.70) | copy-start | bytes 3076
  558.4 233.5 %all-to-all-start.2 = ((bf16[64,1,128,224]{2,3,1,0:T(8,128)(2,1)}), bf16[64,1,128,224]{2,3,1,0:T(8,128)(2,1)}, u32[]{:S(2)}, u32[]{:S(2)}) async-start(bf16[64,1,128,224]{2,3,1,0:T(8,128)(2,1)} %bitcast.117), calls=%async_computation.4 | async-start | bytes 7340032 | tf_op jit(solution)/shard_map/all_to_all | solution.py:113
  815.9 27.4 %copy-start.1 = (s32[1024]{0:T(1024)S(1)}, s32[1024]{0:T(1024)}, u32[]{:S(2)}) copy-start(s32[1024]{0:T(1024)} %param.11) | copy-start | bytes 12292
Sparse Core Ops, SparseCore 0:
  10.4 50.0 all-gather.1
  507.0 46.1 reduce-scatter.4
  556.7 233.6 all-reduce.2
  793.3 49.8 reduce-scatter.2
where the time goes:
time: 857 us; the launch traced here: 850 us
  waiting for transfers between devices  594 us (69%)
  local copies, waits for them, and re-layouts  102 us (12%)
  matrix products  76 us (9%)
  starting transfers between devices  22.5 us (3%)
  blocking collectives  22.2 us (3%)
  other arithmetic  18.5 us (2%)
  between operations  15 us (2%)
    all_to_all x1, waiting for transfers between devices, shards(): lax.all_to_all(packed, 'dp', split_axis=0, concat_axis=0, tiled=True)  317 us
    unnamed x5, waiting for transfers between devices  220 us
    all_gather x1, waiting for transfers between devices, shards(): whole_own = lax.all_gather(encodings, 'head', axis=2, tiled=True)  24.8 us
    all_to_all x1, blocking collectives, shards(): lax.all_to_all(requests, 'dp', split_axis=0, concat_axis=0, tiled=True)  22.2 us
    dot_general x1, matrix products, shards(): jnp.einsum('chqk,cqhd->ckhd', grad_scores, query_heads, preferred_element...  17.2 us
  transfers between devices with their start and end apart: 6, of which 5 were waited for; matrix products, arithmetic and copies ran while one was open for 9% of the time, Pallas kernels for 0%

commit v1 on v0

--- a/solution.py
+++ b/solution.py
@@ -9,6 +9,13 @@
 CH = 64
 NTOK = 128
 NEIGH = 2
+
+
+def deliver_column_now(original, mesh_dim):
+    low = jnp.stack([original for _ in range(lax.axis_size(mesh_dim))])
+    newest = lax.all_to_all(low, mesh_dim, split_axis=0, concat_axis=0)
+    row_out = jnp.concatenate(newest, 2)
+    return row_out
 
 
 def shards(
@@ -44,7 +51,7 @@
     valid_mask = asked_rows >= 0
     local_index = jnp.maximum(asked_rows, 0)
     blank = jnp.zeros((), jnp.bfloat16)
-    whole_own = lax.all_gather(encodings, "head", axis=2, tiled=True)
+    whole_own = deliver_column_now(encodings, mesh_dim="head")
     packed = jnp.where(valid_mask[:, :, None, None], whole_own[local_index], blank)
     received = lax.all_to_all(packed, "dp", split_axis=0, concat_axis=0, tiled=True)
     slot_blocks = received[owner_dev, slot_rank]

time: 857 us -> 812 us (0.947)
  waiting for transfers between devices: 594 us -> 526 us
  local copies, waits for them, and re-layouts: 102 us -> 122 us
    unnamed x5 -> x4, waiting for transfers between devices: 220 us -> 155 us
    all_to_all x0 -> x1, waiting for transfers between devices: none -> 40.2 us  [deliver_column_now(): newest = lax.all_to_all(low, mesh_dim, split_axis=0, concat_axis=0)]
    all_gather x1 -> x0, waiting for transfers between devices: 24.8 us -> none  [shards(): whole_own = lax.all_gather(encodings, 'head', axis=2, tiled=True)]
    all_to_all x0 -> x2, local copies, waits for them, and re-layouts: none -> 24.2 us  [the longest x1 20 us: shards(): lax.all_to_all(packed, 'dp', split_axis=0, concat_axis=0, tiled=True)]
    reduce_scatter x1, waiting for transfers between devices: 16.9 us -> 0.01 us  [shards(): lax.psum_scatter(partial_input.astype(jnp.bfloat16), 'head', scatter_dime...]
  transfers between devices with their start and end apart: 6 -> 6, of which waited for: 5 -> 4; matrix products, arithmetic and copies ran while one was open for 9% -> 10% of each run, Pallas kernels for 0% -> 0%
where the time goes in v1:
time: 812 us; the launch traced here: 803 us
  waiting for transfers between devices  526 us (65%)
  local copies, waits for them, and re-layouts  122 us (15%)
  matrix products  75.6 us (9%)
  starting transfers between devices  23 us (3%)
  blocking collectives  22.2 us (3%)
  other arithmetic  18.1 us (2%)
  between operations  16.6 us (2%)
    all_to_all x1, waiting for transfers between devices, shards(): lax.all_to_all(packed, 'dp', split_axis=0, concat_axis=0, tiled=True)  316 us
    unnamed x4, waiting for transfers between devices  155 us
    all_to_all x1, waiting for transfers between devices, deliver_column_now(): newest = lax.all_to_all(low, mesh_dim, split_axis=0, concat_axis=0)  40.2 us
    all_to_all x1, blocking collectives, shards(): lax.all_to_all(requests, 'dp', split_axis=0, concat_axis=0, tiled=True)  22.2 us
    all_to_all x1, local copies, waits for them, and re-layouts, shards(): lax.all_to_all(packed, 'dp', split_axis=0, concat_axis=0, tiled=True)  20 us
    dot_general x1, matrix products, shards(): jnp.einsum('chqk,cqhd->ckhd', grad_scores, query_heads, preferred_element...  17 us
  transfers between devices with their start and end apart: 6, of which 4 were waited for; matrix products, arithmetic and copies ran while one was open for 10% of the time, Pallas kernels for 0%

profile of v1, /device:TPU:1, one launch (start us, length us, event | category | flops | bytes accessed | tf_op | source)
XLA Modules:
  0.0 803.4 jit_solution(2565675848225149839)
XLA Ops:
  8.0 0.8 copy.93
  8.8 0.1 reshape.345
  8.9 0.6 gather_fusion
  9.5 0.2 convert_reduce_fusion
  9.7 0.1 select_reduce_fusion
  9.8 0.1 copy.94
  9.9 22.2 %all_to_all.21 = s32[64,1,1]{2,1,0:T(1,128)S(1)} all-to-all(s32[64,1,1]{2,1,0:T(1,128)S(1)} %copy.94), channel_id=1, replica_groups=mesh['dp'=64,'head'=4] {'dp'}, dimensions={0} | all-to-all | bytes 512 | tf_op jit(solution)/shard_map/all_to_all | solution.py:50
  32.1 3.6 stack.2
  35.7 4.7 all-to-all-start.1
  40.4 1.2 maximum_reduce_fusion
  41.7 1.2 compare_reduce_fusion
  42.9 40.2 %all-to-all-done.1 = bf16[4,16,128,224]{2,3,1,0:T(8,128)(2,1)} async-done(((bf16[4,16,128,224]{2,3,1,0:T(8,128)(2,1)}), bf16[4,16,128,224]{2,3,1,0:T(8,128)(2,1)}, u32[]{:S(2)}, u32[]{:S(2)}) %all-to-all-start.1) | async-done | bytes 3670048 | tf_op jit(solution)/shard_map/all_to_all | solution.py:16
  83.1 4.3 copy.95
  87.4 9.8 %gather_fusion.1 = bf16[64,128,896]{1,2,0:T(8,128)(2,1)} fusion(bf16[16,128,896]{1,2,0:T(8,128)(2,1)} %bitcast.120, s32[1024]{0:T(1024)S(1)} %pad_clamp_fusion), kind=kCustom, calls=%fused_computation.1 | custom fusion | bytes 29360384 | tf_op jit(solution)/shard_map/gather | solution.py:55
  97.2 13.4 %fusion.2 = bf16[64,1,128,896]{2,3,1,0:T(8,128)(2,1)} fusion(bf16[64,128,896]{1,2,0:T(8,128)(2,1)} %gather_fusion.1, pred[64]{0:T(512)(128)(4,1)S(1)} %compare_reduce_fusion), kind=kLoop, calls=%fused_computation.7 | loop fusion | flops 7340032 | bytes 29360192 | tf_op jit(solution)/shard_map/jit(_where)/select_n | solution.py:55
  110.6 6.8 all-to-all-start.2
  117.5 0.0 reduce-scatter.5.cloned.1.call-start
  117.5 0.1 reshape.350
  117.7 1.3 reshape.352
  119.0 0.1 constant_dynamic-update-slice_fusion.1
  119.1 0.1 constant_dynamic-update-slice_fusion
  119.2 1.3 copy-done.9
  120.5 316.0 %all-to-all-done.2 = bf16[64,1,128,896]{2,3,1,0:T(8,128)(2,1)} async-done(((bf16[64,1,128,896]{2,3,1,0:T(8,128)(2,1)}), bf16[64,1,128,896]{2,3,1,0:T(8,128)(2,1)}, u32[]{:S(2)}, u32[]{:S(2)}) %all-to-all-start.2) | async-done | bytes 14680096 | tf_op jit(solution)/shard_map/all_to_all | solution.py:56
  436.5 20.0 %copy.97 = bf16[64,1,128,896]{3,2,1,0:T(8,128)(2,1)} copy(bf16[64,1,128,896]{2,3,1,0:T(8,128)(2,1)} %all-to-all-done.2) | data formatting | bytes 29360128 | tf_op jit(solution)/shard_map/all_to_all | solution.py:56
  456.5 8.1 %gather_fusion.2 = bf16[16,128,896]{2,1,0:T(8,128)(2,1)} fusion(bf16[64,1,128,896]{3,2,1,0:T(8,128)(2,1)} %copy.97, s32[16]{0:T(128)S(1)} %get-tuple-element.33), kind=kCustom, calls=%fused_computation.2 | custom fusion | bytes 7340160 | tf_op jit(solution)/shard_map/gather | solution.py:57
  464.6 6.8 convolution_convert_fusion.1
  471.4 2.2 fusion.51
  473.7 2.5 reshape.349
  476.2 0.8 fusion.13
  477.1 1.9 fusion.53
  479.0 4.0 reshape.351
  483.0 3.8 fusion.8
  486.8 7.9 convert_bitcast_fusion
  494.7 17.0 %convert_bitcast_fusion.1 = bf16[8,256,4,128]{3,1,2,0:T(8,128)(2,1)} fusion(f32[8,4,256,64]{2,3,1,0:T(8,128)} %fusion.8, bf16[8,64,4,128]{3,2,1,0:T(4,128)(2,1)S(1)} %reshape.350, f32[8,4,64,256]{3,2,1,0:T(8,128)} %get-tuple-element.37, f32[8,4,64]{2,1,0:T(4,128)S(1)} %get-tuple-element.36), kind=kOutput, calls=%fused_computation.23 | convolution fusion | flops 138938624 | bytes 6823936 | tf_op jit(solution)/shard_map/chqk,cqhd->ckhd/dot_general | solution.py:85
  511.7 4.5 copy.105
  516.2 2.3 copy.114
  518.5 1.5 constant_dynamic-update-slice_fusion.3
  520.0 4.6 copy.107
  524.7 2.4 copy.115
  527.1 0.4 copy-done.4
  527.5 0.1 constant_dynamic-update-slice_fusion.2
  527.6 1.4 copy-done.11
  529.0 6.0 convolution_convert_fusion.2
  535.0 6.1 copy.108
  541.1 0.0 all-reduce.3.cloned.1.call-start
  541.2 9.2 %fusion.54 = f32[896,1024]{1,0:T(8,128)} fusion(bf16[2048,896]{1,0:T(8,128)(2,1)} %bitcast.129, bf16[2048,1024]{0,1:T(8,128)(2,1)} %copy-done.5), kind=kOutput, calls=%fused_computation.90 | convolution fusion | flops 3758096384 | bytes 11534336 | tf_op jit(solution)/shard_map/dot_general | solution.py:101
  550.4 0.0 all-reduce.3.cloned.1.call-update
  550.4 0.3 reduce-scatter.3.cloned.1.call-start
  550.7 14.7 %fusion.20 = bf16[8,64,4,128]{3,1,2,0:T(8,128)(2,1)S(1)} fusion(bf16[8,256,4,128]{3,2,1,0:T(4,128)(2,1)S(1)} %reshape.349, f32[8,4,256,64]{2,3,1,0:T(8,128)} %fusion.8, f32[8,4,64,256]{3,2,1,0:T(8,128)} %get-tuple-element.37, f32[8,4,64]{2,1,0:T(4,128)S(1)} %get-tuple-element.36), kind=kOutput, calls=%fused_computation.31 | convolution fusion | flops 138152192 | bytes 6823936 | tf_op jit(solution)/shard_map/chqk,ckhd->cqhd/dot_general | solution.py:88
  565.4 0.4 copy.103
  565.9 6.6 convolution_convert_fusion
  572.5 15.2 %reduce-scatter.5.cloned.1.call-done = bf16[16,128,224]{1,2,0:T(8,128)(2,1)} async-done(((bf16[16,128,896]{1,2,0:T(8,128)(2,1)}), bf16[16,128,224]{1,2,0:T(8,128)(2,1)}) %reduce-scatter.5.cloned.1.call-update) | async-done | bytes 917520 | tf_op jit(solution)/shard_map/reduce_scatter | solution.py:111
  587.7 2.3 broadcast.390
  589.9 2.9 scatter_fusion
  592.9 11.1 %all-to-all-start.3 = ((bf16[64,1,128,224]{2,3,1,0:T(8,128)(2,1)}), bf16[64,1,128,224]{2,3,1,0:T(8,128)(2,1)}, u32[]{:S(2)}, u32[]{:S(2)}) async-start(bf16[64,1,128,224]{2,3,1,0:T(8,128)(2,1)} %bitcast.121), calls=%async_computation.5 | async-start | bytes 7340032 | tf_op jit(solution)/shard_map/all_to_all | solution.py:120
  604.0 0.6 dynamic-slice
  605.2 154.7 %all-reduce.3.cloned.1.call-done = f32[896,1024]{1,0:T(8,128)} async-done(((f32[896,1024]{1,0:T(8,128)}), f32[896,1024]{1,0:T(8,128)}) %all-reduce.3.cloned.1.call-update) | async-done | bytes 3670032
  759.9 1.5 fusion.52
  761.5 6.2 copy.110
  767.7 9.7 %reshape.356 = bf16[64,28672]{1,0:T(8,128)(2,1)} reshape(bf16[64,1,128,224]{3,2,0,1:T(8,128)(2,1)} %copy.110) | data formatting | bytes 7340032 | tf_op jit(solution)/shard_map/reshape | solution.py:126
  777.4 8.0 dot_general.46
  785.4 6.5 copy.111
  792.0 2.6 convolution_convert_fusion.3
  794.6 1.2 copy.112
  (34 shorter events, 0.2 us)
Async XLA Ops:
  8.0 0.9 copy-start
  35.7 47.4 %all-to-all-start.1 = ((bf16[4,16,128,224]{2,3,1,0:T(8,128)(2,1)}), bf16[4,16,128,224]{2,3,1,0:T(8,128)(2,1)}, u32[]{:S(2)}, u32[]{:S(2)}) async-start(bf16[4,16,128,224]{2,3,1,0:T(8,128)(2,1)} %stack.2), calls=%async_computation.1 | async-start | bytes 7340032 | tf_op jit(solution)/shard_map/all_to_all | solution.py:16
  110.6 6.9 copy-start.8
  110.6 325.9 %all-to-all-start.2 = ((bf16[64,1,128,896]{2,3,1,0:T(8,128)(2,1)}), bf16[64,1,128,896]{2,3,1,0:T(8,128)(2,1)}, u32[]{:S(2)}, u32[]{:S(2)}) async-start(bf16[64,1,128,896]{2,3,1,0:T(8,128)(2,1)} %fusion.2), calls=%async_computation.2 | async-start | bytes 29360128 | tf_op jit(solution)/shard_map/all_to_all | solution.py:56
  117.5 1.5 copy-start.6
  117.5 1.6 copy-start.7
  117.5 470.2 %reduce-scatter.5.cloned.1.call-start = ((), (), s32[]{:S(2)}) async-start(), calls=%async_computation.7 | async-start | bytes 4587520 | tf_op jit(solution)/shard_map/reduce_scatter | solution.py:111
  119.2 1.3 copy-start.9
  456.5 8.1 %copy-start.10 = (bf16[896,1024]{1,0:T(8,128)(2,1)S(1)}, bf16[896,1024]{1,0:T(8,128)(2,1)}, u32[]{:S(2)}) copy-start(bf16[896,1024]{1,0:T(8,128)(2,1)} %copy-done.9) | copy-start | bytes 5505028
  477.1 2.0 copy-start.2
  524.7 2.8 copy-start.4
  527.5 1.5 copy-start.11
  529.0 6.0 copy-start.5
  541.1 218.8 %all-reduce.3.cloned.1.call-start = ((), (), s32[]{:S(2)}) async-start(), calls=%async_computation.8 | async-start | bytes 7340032
  550.4 245.3 %reduce-scatter.3.cloned.1.call-start = ((), (), s32[]{:S(2)}) async-start(), calls=%async_computation.6 | async-start | bytes 5242880 | tf_op jit(solution)/shard_map/reduce_scatter | solution.py:94
  587.6 2.3 copy-start.3
  592.9 11.1 %copy-start.12 = (u32[256]{0:T(256)S(1)}, u32[256]{0:T(256)}, u32[]{:S(2)}) copy-start(u32[256]{0:T(256)} %constant.70) | copy-start | bytes 3076
  592.9 168.6 %all-to-all-start.3 = ((bf16[64,1,128,224]{2,3,1,0:T(8,128)(2,1)}), bf16[64,1,128,224]{2,3,1,0:T(8,128)(2,1)}, u32[]{:S(2)}, u32[]{:S(2)}) async-start(bf16[64,1,128,224]{2,3,1,0:T(8,128)(2,1)} %bitcast.121), calls=%async_computation.5 | async-start | bytes 7340032 | tf_op jit(solution)/shard_map/all_to_all | solution.py:120
  785.4 10.3 %copy-start.1 = (s32[1024]{0:T(1024)S(1)}, s32[1024]{0:T(1024)}, u32[]{:S(2)}) copy-start(s32[1024]{0:T(1024)} %param.11) | copy-start | bytes 12292
Sparse Core Ops, SparseCore 0:
  541.2 46.3 reduce-scatter.4
  590.8 49.1 reduce-scatter.2
Sparse Core Ops, SparseCore 1:
  550.5 209.4 all-reduce.2
